TPU v7x, 32 devices: a whole 2x2x4 slice. The times are simulated.
32 devices in a mesh: sect: 2 (over x), slab: 8 (over z, y), energy: 2 (over core).
Axes of the slice: x: 2, y: 2, z: 4, core: 2. Of those that a mesh axis runs over, the one named last changes fastest.
Arguments:
- source: bfloat16 [4, 512, 128], P(('energy', 'sect'), 'slab'), parts along dimension 0, may hold values from -6 to 6
- forward_mult: bfloat16 [4, 2, 512, 512], P(('energy', 'sect'), None, 'slab'), parts along dimension 0, may hold values from -0.1875 to 0.1875
- schur_inverse: bfloat16 [4, 2, 512, 512], P(('energy', 'sect'), None, 'slab'), parts along dimension 0, may hold values from -0.09375 to 0.09375
- upper_mult: bfloat16 [4, 2, 512, 512], P(('energy', 'sect'), None, 'slab'), parts along dimension 0, may hold values from -0.125 to 0.125
Outputs:
- wave: bfloat16 [4, 512, 128], P(('energy', 'sect'), 'slab'), parts along dimension 0
There are 2 independent parts, one for each index of `energy`. A program takes and returns all parts, laid end to end along the dimension named above; each array names one. Nothing has to cross between parts.
All inputs are finite; a program needn't handle non-finite values.
Results may differ from a plain program's by a relative error of at most 0.012.
Values may be sent and summed in bfloat16 or wider, within the bound.
No kernel may reach another device: no remote copies, remote signals or barrier semaphores. Data moves between devices by JAX's collectives and lax.ppermute only.
A program may use at most 64 MiB of HBM per device.

v0:
```python
import jax
import jax.numpy as jnp
from jax import lax
from jax.sharding import PartitionSpec as P


def from_behind(block, axis, distance):
    devices = range(lax.axis_size(axis))
    route = [(i - distance, i) for i in devices if i - distance in devices]
    return lax.ppermute(block, axis, route)


def complex_apply(matrix, vector):
    half_cols = vector.shape[1] // 2
    real_part = jnp.dot(matrix[0], vector, preferred_element_type=jnp.float32)
    imag_part = jnp.dot(matrix[1], vector, preferred_element_type=jnp.float32)
    return jnp.concatenate(
        [
            real_part[:, :half_cols] - imag_part[:, half_cols:],
            real_part[:, half_cols:] + imag_part[:, :half_cols],
        ],
        axis=1,
    )


def fold_rows(matrix, rows_in):
    return complex_apply(matrix, rows_in)


def per_device(source, forward_mult, schur_inverse, upper_mult):
    local_src = source[0]
    forward_local = forward_mult[0]
    inverse_local = schur_inverse[0]
    upper_local = upper_mult[0]
    sections = lax.axis_size("sect")
    src_float = local_src.astype(jnp.float32)

    def forward_segment(segment_no, current):
        inflow = from_behind(current, "sect", 1)
        summed = fold_rows(forward_local, lax.all_gather(inflow, "slab", axis=0, tiled=True))
        return (src_float + summed).astype(jnp.bfloat16)

    forward_rows = lax.fori_loop(0, sections, forward_segment, local_src)
    scaled = fold_rows(inverse_local, lax.all_gather(forward_rows, "slab", axis=0, tiled=True))

    def backward_segment(segment_no, current):
        outflow = from_behind(current, "sect", -1)
        summed = fold_rows(upper_local, lax.all_gather(outflow, "slab", axis=0, tiled=True))
        return (scaled - summed).astype(jnp.bfloat16)

    wave_rows = lax.fori_loop(0, sections, backward_segment, scaled.astype(jnp.bfloat16))
    return wave_rows[None]


def solution(mesh):
    in_specs = (
        P(("energy", "sect"), "slab", None),
        P(("energy", "sect"), None, "slab", None),
        P(("energy", "sect"), None, "slab", None),
        P(("energy", "sect"), None, "slab", None),
    )
    out_specs = P(("energy", "sect"), "slab", None)
    return jax.shard_map(
        per_device, mesh=mesh, in_specs=in_specs, out_specs=out_specs, check_vma=False
    )
```

profile of v0, /device:TPU:0, one launch (start us, length us, event | category | flops | bytes accessed | tf_op | source)
XLA Modules:
  0.0 181.1 jit_solution(12969878950898552480)
XLA Ops:
  0.0 0.7 copy.19
  0.7 74.7 %while.20 = (s32[]{:T(128)}, bf16[64,128]{1,0:T(8,128)(2,1)S(1)}, bf16[2,64,512]{2,1,0:T(8,128)(2,1)}, f32[64,128]{1,0:T(8,128)S(1)}, s32[]{:T(128)}) while((s32[]{:T(128)}, bf16[64,128]{1,0:T(8,128)(2,1)S(1)}, bf16[2,64,512]{2,1,0:T(8,128)(2,1)}, f32[64,128]{1,0:T(8,128)S(1)}, s32[]{:T(128)}) %tuple.47), condition=%wide.region_1.0_spmd, body=%wide.region_0.0_spmd.sunk | while | flops 16809984 | bytes 1376385 | solution.py:43
  0.7 5.0 %collective-permute-start = (bf16[64,128]{1,0:T(8,128)(2,1)S(1)}, bf16[64,128]{1,0:T(8,128)(2,1)S(1)}, u32[]{:S(2)}, u32[]{:S(2)}) collective-permute-start(bf16[64,128]{1,0:T(8,128)(2,1)S(1)} %get-tuple-element.139), channel_id=1, source_target_pairs={{0,16},{1,17},{2,18},{3,19},{4,20},{5,21},{6,22},{7,23},{8,24},{9,... | collective-permute-start | bytes 49160 | tf_op jit(solution)/shard_map/while/body/eval_jaxpr/ppermute | solution.py:10
  5.7 1.4 collective-permute-done
  7.2 30.8 %all_gather.12 = bf16[512,128]{1,0:T(8,128)(2,1)S(1)} all-gather(bf16[64,128]{1,0:T(8,128)(2,1)S(1)} %collective-permute-done), channel_id=1, replica_groups=mesh['sect'=2,'slab'=8,'energy'=2] {'slab'}, dimensions={0}, use_global_device_ids=true | all-gather | bytes 147456 | tf_op jit(solution)/shard_map/while/body/eval_jaxpr/all_gather | solution.py:40
  38.0 0.2 fusion.44
  38.2 0.2 fusion.43
  38.3 0.1 slice_subtract_fusion.5
  38.5 4.4 %collective-permute-start = (bf16[64,128]{1,0:T(8,128)(2,1)S(1)}, bf16[64,128]{1,0:T(8,128)(2,1)S(1)}, u32[]{:S(2)}, u32[]{:S(2)}) collective-permute-start(bf16[64,128]{1,0:T(8,128)(2,1)S(1)} %get-tuple-element.139), channel_id=1, source_target_pairs={{0,16},{1,17},{2,18},{3,19},{4,20},{5,21},{6,22},{7,23},{8,24},{9,... | collective-permute-start | bytes 49160 | tf_op jit(solution)/shard_map/while/body/eval_jaxpr/ppermute | solution.py:10
  42.9 1.4 collective-permute-done
  44.3 30.6 %all_gather.12 = bf16[512,128]{1,0:T(8,128)(2,1)S(1)} all-gather(bf16[64,128]{1,0:T(8,128)(2,1)S(1)} %collective-permute-done), channel_id=1, replica_groups=mesh['sect'=2,'slab'=8,'energy'=2] {'slab'}, dimensions={0}, use_global_device_ids=true | all-gather | bytes 147456 | tf_op jit(solution)/shard_map/while/body/eval_jaxpr/all_gather | solution.py:40
  74.9 0.2 fusion.44
  75.1 0.2 fusion.43
  75.2 0.1 slice_subtract_fusion.5
  75.4 30.7 %all_gather.9 = bf16[512,128]{1,0:T(8,128)(2,1)S(1)} all-gather(bf16[64,128]{1,0:T(8,128)(2,1)S(1)} %get-tuple-element.49), channel_id=1, replica_groups=mesh['sect'=2,'slab'=8,'energy'=2] {'slab'}, dimensions={0}, use_global_device_ids=true | all-gather | bytes 147456 | tf_op jit(solution)/shard_map/all_gather | solution.py:44
  106.1 0.2 convolution_bitcast_fusion.1
  106.2 0.2 convolution_bitcast_fusion
  106.6 0.7 copy-done.1
  107.3 73.2 %while.21 = (s32[]{:T(128)}, bf16[64,128]{1,0:T(8,128)(2,1)S(1)}, bf16[2,64,512]{2,1,0:T(8,128)(2,1)S(1)}, f32[64,128]{1,0:T(8,128)S(1)}, s32[]{:T(128)}) while((s32[]{:T(128)}, bf16[64,128]{1,0:T(8,128)(2,1)S(1)}, bf16[2,64,512]{2,1,0:T(8,128)(2,1)S(1)}, f32[64,128]{1,0:T(8,128)S(1)}, s32[]{:T(128)}) %tuple.46), condition=%wide.region_3.0_spmd, body=%wide.region_2.0_spmd.sunk | while | flops 16809984 | bytes 852069 | solution.py:51
  107.3 1.3 collective-permute-start.1
  108.6 4.3 %collective-permute-done.1 = bf16[64,128]{1,0:T(8,128)(2,1)S(1)} collective-permute-done((bf16[64,128]{1,0:T(8,128)(2,1)S(1)}, bf16[64,128]{1,0:T(8,128)(2,1)S(1)}, u32[]{:S(2)}, u32[]{:S(2)}) %collective-permute-start.1) | collective-permute-done | bytes 16416 | tf_op jit(solution)/shard_map/while/body/eval_jaxpr/ppermute | solution.py:10
  112.9 30.5 %all_gather.13 = bf16[512,128]{1,0:T(8,128)(2,1)S(1)} all-gather(bf16[64,128]{1,0:T(8,128)(2,1)S(1)} %collective-permute-done.1), channel_id=1, replica_groups=mesh['sect'=2,'slab'=8,'energy'=2] {'slab'}, dimensions={0}, use_global_device_ids=true | all-gather | bytes 147456 | tf_op jit(solution)/shard_map/while/body/eval_jaxpr/all_gather | solution.py:48
  143.4 0.2 fusion.51
  143.6 0.2 fusion.50
  143.7 0.1 slice_subtract_fusion.6
  143.9 1.3 collective-permute-start.1
  145.2 4.3 %collective-permute-done.1 = bf16[64,128]{1,0:T(8,128)(2,1)S(1)} collective-permute-done((bf16[64,128]{1,0:T(8,128)(2,1)S(1)}, bf16[64,128]{1,0:T(8,128)(2,1)S(1)}, u32[]{:S(2)}, u32[]{:S(2)}) %collective-permute-start.1) | collective-permute-done | bytes 16416 | tf_op jit(solution)/shard_map/while/body/eval_jaxpr/ppermute | solution.py:10
  149.5 30.5 %all_gather.13 = bf16[512,128]{1,0:T(8,128)(2,1)S(1)} all-gather(bf16[64,128]{1,0:T(8,128)(2,1)S(1)} %collective-permute-done.1), channel_id=1, replica_groups=mesh['sect'=2,'slab'=8,'energy'=2] {'slab'}, dimensions={0}, use_global_device_ids=true | all-gather | bytes 147456 | tf_op jit(solution)/shard_map/while/body/eval_jaxpr/all_gather | solution.py:48
  180.1 0.2 fusion.51
  180.2 0.2 fusion.50
  180.4 0.1 slice_subtract_fusion.6
  180.5 0.6 copy-done.3
  (15 shorter events, 0.5 us)
Async XLA Ops:
  0.7 37.3 %copy-start = (bf16[2,64,512]{2,1,0:T(8,128)(2,1)S(1)}, bf16[2,64,512]{2,1,0:T(8,128)(2,1)}, u32[]{:S(2)}) copy-start(bf16[2,64,512]{2,1,0:T(8,128)(2,1)} %get-tuple-element.145) | copy-start | bytes 393220 | tf_op jit(solution)/shard_map/while
  0.7 6.4 %collective-permute-start = (bf16[64,128]{1,0:T(8,128)(2,1)S(1)}, bf16[64,128]{1,0:T(8,128)(2,1)S(1)}, u32[]{:S(2)}, u32[]{:S(2)}) collective-permute-start(bf16[64,128]{1,0:T(8,128)(2,1)S(1)} %get-tuple-element.139), channel_id=1, source_target_pairs={{0,16},{1,17},{2,18},{3,19},{4,20},{5,21},{6,22},{7,23},{8,24},{9,... | collective-permute-start | bytes 49160 | tf_op jit(solution)/shard_map/while/body/eval_jaxpr/ppermute | solution.py:10
  38.5 36.4 %copy-start = (bf16[2,64,512]{2,1,0:T(8,128)(2,1)S(1)}, bf16[2,64,512]{2,1,0:T(8,128)(2,1)}, u32[]{:S(2)}) copy-start(bf16[2,64,512]{2,1,0:T(8,128)(2,1)} %get-tuple-element.145) | copy-start | bytes 393220 | tf_op jit(solution)/shard_map/while
  38.5 5.8 %collective-permute-start = (bf16[64,128]{1,0:T(8,128)(2,1)S(1)}, bf16[64,128]{1,0:T(8,128)(2,1)S(1)}, u32[]{:S(2)}, u32[]{:S(2)}) collective-permute-start(bf16[64,128]{1,0:T(8,128)(2,1)S(1)} %get-tuple-element.139), channel_id=1, source_target_pairs={{0,16},{1,17},{2,18},{3,19},{4,20},{5,21},{6,22},{7,23},{8,24},{9,... | collective-permute-start | bytes 49160 | tf_op jit(solution)/shard_map/while/body/eval_jaxpr/ppermute | solution.py:10
  75.4 30.7 %copy-start.2 = (bf16[1,2,64,512]{3,2,1,0:T(8,128)(2,1)S(1)}, bf16[1,2,64,512]{3,2,1,0:T(8,128)(2,1)}, u32[]{:S(2)}) copy-start(bf16[1,2,64,512]{3,2,1,0:T(8,128)(2,1)} %param.10) | copy-start | bytes 393220
  106.4 0.9 copy-start.1
  107.3 5.6 %collective-permute-start.1 = (bf16[64,128]{1,0:T(8,128)(2,1)S(1)}, bf16[64,128]{1,0:T(8,128)(2,1)S(1)}, u32[]{:S(2)}, u32[]{:S(2)}) collective-permute-start(bf16[64,128]{1,0:T(8,128)(2,1)S(1)} %get-tuple-element.154), channel_id=1, source_target_pairs={{16,0},{17,1},{18,2},{19,3},{20,4},{21,5},{22,6},{23,7},{24,8},{25... | collective-permute-start | bytes 49160 | tf_op jit(solution)/shard_map/while/body/eval_jaxpr/ppermute | solution.py:10
  143.9 5.6 %collective-permute-start.1 = (bf16[64,128]{1,0:T(8,128)(2,1)S(1)}, bf16[64,128]{1,0:T(8,128)(2,1)S(1)}, u32[]{:S(2)}, u32[]{:S(2)}) collective-permute-start(bf16[64,128]{1,0:T(8,128)(2,1)S(1)} %get-tuple-element.154), channel_id=1, source_target_pairs={{16,0},{17,1},{18,2},{19,3},{20,4},{21,5},{22,6},{23,7},{24,8},{25... | collective-permute-start | bytes 49160 | tf_op jit(solution)/shard_map/while/body/eval_jaxpr/ppermute | solution.py:10
  180.5 0.6 copy-start.3
where the time goes:
time: 181 us
  blocking collectives  153 us (85%)
  starting transfers between devices  12 us (7%)
  waiting for transfers between devices  11.5 us (6%)
  local copies, waits for them, and re-layouts  2.07 us (1%)
    all_gather x2, blocking collectives, forward_segment(): lax.all_gather(inflow, 'slab', axis=0, tiled=True)  61.4 us
    all_gather x2, blocking collectives, backward_segment(): lax.all_gather(outflow, 'slab', axis=0, tiled=True)  61 us
    all_gather x1, blocking collectives, per_device(): lax.all_gather(forward_rows, 'slab', axis=0, tiled=True)  30.7 us
    ppermute x4, starting transfers between devices, from_behind(): return lax.ppermute(block, axis, route)  12 us
    ppermute x4, waiting for transfers between devices, from_behind(): return lax.ppermute(block, axis, route)  11.5 us
  transfers between devices with their start and end apart: 4, of which 4 were waited for; matrix products, arithmetic and copies ran while one was open for 0% of the time, Pallas kernels for 0%

commit v1 on v0

--- a/solution.py
+++ b/solution.py
@@ -2,6 +2,27 @@
 import jax.numpy as jnp
 from jax import lax
 from jax.sharding import PartitionSpec as P
+
+
+def post_the_region(local, dim_k):
+    vec_out = list(local.shape[1:])
+    vec_out[dim_k] *= local.shape[0]
+    return jnp.moveaxis(local, 0, dim_k).reshape(vec_out)
+
+
+def post_the_windows(in_array, along_axis):
+    newest, local_next = (lax.axis_size(along_axis), lax.axis_index(along_axis))
+    a_next, item_now = (in_array[None], 1)
+    while item_now < newest:
+        block_out = lax.ppermute(
+            a_next, along_axis, tuple(((to_i, to_i ^ item_now) for to_i in range(newest)))
+        )
+        state_next = local_next & item_now == 0
+        a_next = jnp.concatenate(
+            [jnp.where(state_next, a_next, block_out), jnp.where(state_next, block_out, a_next)]
+        )
+        item_now *= 2
+    return a_next
 
 
 def from_behind(block, axis, distance):
@@ -41,7 +62,11 @@
         return (src_float + summed).astype(jnp.bfloat16)
 
     forward_rows = lax.fori_loop(0, sections, forward_segment, local_src)
-    scaled = fold_rows(inverse_local, lax.all_gather(forward_rows, "slab", axis=0, tiled=True))
+
+    def manage_the_lanes(message, frame_in, out_dim=0):
+        return post_the_region(post_the_windows(message, frame_in), out_dim)
+
+    scaled = fold_rows(inverse_local, manage_the_lanes(forward_rows, frame_in="slab"))
 
     def backward_segment(segment_no, current):
         outflow = from_behind(current, "sect", -1)

time: 181 us -> 165 us (0.912)
  blocking collectives: 153 us -> 122 us
  waiting for transfers between devices: 11.5 us -> 22 us
  starting transfers between devices: 12 us -> 14.9 us
    all_gather x1 -> x0, blocking collectives: 30.7 us -> none  [per_device(): lax.all_gather(forward_rows, 'slab', axis=0, tiled=True)]
    ppermute x0 -> x3, waiting for transfers between devices: none -> 10.5 us  [post_the_windows(): lax.ppermute(a_next, along_axis, tuple(((to_i, to_i ^ item_now) for to_i...]
    ppermute x0 -> x3, starting transfers between devices: none -> 2.97 us  [post_the_windows(): lax.ppermute(a_next, along_axis, tuple(((to_i, to_i ^ item_now) for to_i...]
  transfers between devices with their start and end apart: 4 -> 7, of which waited for: 4 -> 7; matrix products, arithmetic and copies ran while one was open for 0% -> 0% of each run, Pallas kernels for 0% -> 0%
where the time goes in v1:
time: 165 us
  blocking collectives  122 us (74%)
  waiting for transfers between devices  22 us (13%)
  starting transfers between devices  14.9 us (9%)
  local copies, waits for them, and re-layouts  2.94 us (2%)
    all_gather x2, blocking collectives, forward_segment(): lax.all_gather(inflow, 'slab', axis=0, tiled=True)  61.4 us
    all_gather x2, blocking collectives, backward_segment(): lax.all_gather(outflow, 'slab', axis=0, tiled=True)  61 us
    ppermute x4, starting transfers between devices, from_behind(): return lax.ppermute(block, axis, route)  12 us
    ppermute x4, waiting for transfers between devices, from_behind(): return lax.ppermute(block, axis, route)  11.5 us
    ppermute x3, waiting for transfers between devices, post_the_windows(): lax.ppermute(a_next, along_axis, tuple(((to_i, to_i ^ item_now) for to_i...  10.5 us
  transfers between devices with their start and end apart: 7, of which 7 were waited for; matrix products, arithmetic and copies ran while one was open for 0% of the time, Pallas kernels for 0%

profile of v1, /device:TPU:0, one launch (start us, length us, event | category | flops | bytes accessed | tf_op | source)
XLA Modules:
  0.0 164.9 jit_solution(6343920039253333578)
XLA Ops:
  0.0 0.7 copy.19
  0.7 74.6 %while.20 = (s32[]{:T(128)}, bf16[64,128]{1,0:T(8,128)(2,1)S(1)}, bf16[2,64,512]{2,1,0:T(8,128)(2,1)}, f32[64,128]{1,0:T(8,128)S(1)}, s32[]{:T(128)}) while((s32[]{:T(128)}, bf16[64,128]{1,0:T(8,128)(2,1)S(1)}, bf16[2,64,512]{2,1,0:T(8,128)(2,1)}, f32[64,128]{1,0:T(8,128)S(1)}, s32[]{:T(128)}) %tuple.50), condition=%wide.region_1.0_spmd, body=%wide.region_0.0_spmd.sunk | while | flops 16809984 | bytes 1376385 | solution.py:64
  0.7 5.0 %collective-permute-start = (bf16[64,128]{1,0:T(8,128)(2,1)S(1)}, bf16[64,128]{1,0:T(8,128)(2,1)S(1)}, u32[]{:S(2)}, u32[]{:S(2)}) collective-permute-start(bf16[64,128]{1,0:T(8,128)(2,1)S(1)} %get-tuple-element.145), channel_id=1, source_target_pairs={{0,16},{1,17},{2,18},{3,19},{4,20},{5,21},{6,22},{7,23},{8,24},{9,... | collective-permute-start | bytes 49160 | tf_op jit(solution)/shard_map/while/body/eval_jaxpr/ppermute | solution.py:31
  5.7 1.4 collective-permute-done
  7.2 30.8 %all_gather.8 = bf16[512,128]{1,0:T(8,128)(2,1)S(1)} all-gather(bf16[64,128]{1,0:T(8,128)(2,1)S(1)} %collective-permute-done), channel_id=1, replica_groups=mesh['sect'=2,'slab'=8,'energy'=2] {'slab'}, dimensions={0}, use_global_device_ids=true | all-gather | bytes 147456 | tf_op jit(solution)/shard_map/while/body/eval_jaxpr/all_gather | solution.py:61
  38.0 0.2 fusion.44
  38.2 0.2 fusion.43
  38.5 4.4 %collective-permute-start = (bf16[64,128]{1,0:T(8,128)(2,1)S(1)}, bf16[64,128]{1,0:T(8,128)(2,1)S(1)}, u32[]{:S(2)}, u32[]{:S(2)}) collective-permute-start(bf16[64,128]{1,0:T(8,128)(2,1)S(1)} %get-tuple-element.145), channel_id=1, source_target_pairs={{0,16},{1,17},{2,18},{3,19},{4,20},{5,21},{6,22},{7,23},{8,24},{9,... | collective-permute-start | bytes 49160 | tf_op jit(solution)/shard_map/while/body/eval_jaxpr/ppermute | solution.py:31
  42.9 1.4 collective-permute-done
  44.3 30.5 %all_gather.8 = bf16[512,128]{1,0:T(8,128)(2,1)S(1)} all-gather(bf16[64,128]{1,0:T(8,128)(2,1)S(1)} %collective-permute-done), channel_id=1, replica_groups=mesh['sect'=2,'slab'=8,'energy'=2] {'slab'}, dimensions={0}, use_global_device_ids=true | all-gather | bytes 147456 | tf_op jit(solution)/shard_map/while/body/eval_jaxpr/all_gather | solution.py:61
  74.9 0.2 fusion.44
  75.0 0.2 fusion.43
  75.4 1.5 collective-permute-start.2
  76.9 2.3 %collective-permute-done.2 = bf16[1,64,128]{2,1,0:T(8,128)(2,1)S(1)} collective-permute-done((bf16[1,64,128]{2,1,0:T(8,128)(2,1)S(1)}, bf16[1,64,128]{2,1,0:T(8,128)(2,1)S(1)}, u32[]{:S(2)}, u32[]{:S(2)}) %collective-permute-start.2) | collective-permute-done | bytes 16416 | tf_op jit(solution)/shard_map/ppermute | solution.py:17
  79.2 3.9 %collective-permute-done.3 = bf16[2,64,128]{2,1,0:T(8,128)(2,1)S(1)} collective-permute-done((bf16[2,64,128]{2,1,0:T(8,128)(2,1)S(1)}, bf16[2,64,128]{2,1,0:T(8,128)(2,1)S(1)}, u32[]{:S(2)}, u32[]{:S(2)}) %collective-permute-start.3) | collective-permute-done | bytes 32800 | tf_op jit(solution)/shard_map/ppermute | solution.py:17
  83.2 1.4 collective-permute-start.4
  84.6 4.3 %collective-permute-done.4 = bf16[4,64,128]{2,1,0:T(8,128)(2,1)S(1)} collective-permute-done((bf16[4,64,128]{2,1,0:T(8,128)(2,1)S(1)}, bf16[4,64,128]{2,1,0:T(8,128)(2,1)S(1)}, u32[]{:S(2)}, u32[]{:S(2)}) %collective-permute-start.4) | collective-permute-done | bytes 65568 | tf_op jit(solution)/shard_map/ppermute | solution.py:17
  88.9 0.9 copy-done.2
  89.8 0.2 convolution_bitcast_fusion.1
  90.0 0.2 convolution_bitcast_fusion
  90.3 0.7 copy-done.1
  91.0 73.3 %while.21 = (s32[]{:T(128)}, bf16[64,128]{1,0:T(8,128)(2,1)S(1)}, bf16[2,64,512]{2,1,0:T(8,128)(2,1)S(1)}, f32[64,128]{1,0:T(8,128)S(1)}, s32[]{:T(128)}) while((s32[]{:T(128)}, bf16[64,128]{1,0:T(8,128)(2,1)S(1)}, bf16[2,64,512]{2,1,0:T(8,128)(2,1)S(1)}, f32[64,128]{1,0:T(8,128)S(1)}, s32[]{:T(128)}) %tuple.49), condition=%wide.region_3.4_spmd, body=%wide.region_2.3_spmd.sunk | while | flops 16809984 | bytes 852069 | solution.py:76
  91.0 1.3 collective-permute-start.1
  92.3 4.3 %collective-permute-done.1 = bf16[64,128]{1,0:T(8,128)(2,1)S(1)} collective-permute-done((bf16[64,128]{1,0:T(8,128)(2,1)S(1)}, bf16[64,128]{1,0:T(8,128)(2,1)S(1)}, u32[]{:S(2)}, u32[]{:S(2)}) %collective-permute-start.1) | collective-permute-done | bytes 16416 | tf_op jit(solution)/shard_map/while/body/eval_jaxpr/ppermute | solution.py:31
  96.6 30.5 %all_gather.9 = bf16[512,128]{1,0:T(8,128)(2,1)S(1)} all-gather(bf16[64,128]{1,0:T(8,128)(2,1)S(1)} %collective-permute-done.1), channel_id=1, replica_groups=mesh['sect'=2,'slab'=8,'energy'=2] {'slab'}, dimensions={0}, use_global_device_ids=true | all-gather | bytes 147456 | tf_op jit(solution)/shard_map/while/body/eval_jaxpr/all_gather | solution.py:73
  127.2 0.2 fusion.51
  127.3 0.2 fusion.50
  127.7 1.3 collective-permute-start.1
  129.0 4.3 %collective-permute-done.1 = bf16[64,128]{1,0:T(8,128)(2,1)S(1)} collective-permute-done((bf16[64,128]{1,0:T(8,128)(2,1)S(1)}, bf16[64,128]{1,0:T(8,128)(2,1)S(1)}, u32[]{:S(2)}, u32[]{:S(2)}) %collective-permute-start.1) | collective-permute-done | bytes 16416 | tf_op jit(solution)/shard_map/while/body/eval_jaxpr/ppermute | solution.py:31
  133.3 30.5 %all_gather.9 = bf16[512,128]{1,0:T(8,128)(2,1)S(1)} all-gather(bf16[64,128]{1,0:T(8,128)(2,1)S(1)} %collective-permute-done.1), channel_id=1, replica_groups=mesh['sect'=2,'slab'=8,'energy'=2] {'slab'}, dimensions={0}, use_global_device_ids=true | all-gather | bytes 147456 | tf_op jit(solution)/shard_map/while/body/eval_jaxpr/all_gather | solution.py:73
  164.0 0.2 fusion.50
  164.3 0.6 copy-done.3
  (26 shorter events, 1.1 us)
Async XLA Ops:
  0.7 37.3 %copy-start = (bf16[2,64,512]{2,1,0:T(8,128)(2,1)S(1)}, bf16[2,64,512]{2,1,0:T(8,128)(2,1)}, u32[]{:S(2)}) copy-start(bf16[2,64,512]{2,1,0:T(8,128)(2,1)} %get-tuple-element.151) | copy-start | bytes 393220 | tf_op jit(solution)/shard_map/while
  0.7 6.4 %collective-permute-start = (bf16[64,128]{1,0:T(8,128)(2,1)S(1)}, bf16[64,128]{1,0:T(8,128)(2,1)S(1)}, u32[]{:S(2)}, u32[]{:S(2)}) collective-permute-start(bf16[64,128]{1,0:T(8,128)(2,1)S(1)} %get-tuple-element.145), channel_id=1, source_target_pairs={{0,16},{1,17},{2,18},{3,19},{4,20},{5,21},{6,22},{7,23},{8,24},{9,... | collective-permute-start | bytes 49160 | tf_op jit(solution)/shard_map/while/body/eval_jaxpr/ppermute | solution.py:31
  38.5 36.4 %copy-start = (bf16[2,64,512]{2,1,0:T(8,128)(2,1)S(1)}, bf16[2,64,512]{2,1,0:T(8,128)(2,1)}, u32[]{:S(2)}) copy-start(bf16[2,64,512]{2,1,0:T(8,128)(2,1)} %get-tuple-element.151) | copy-start | bytes 393220 | tf_op jit(solution)/shard_map/while
  38.5 5.8 %collective-permute-start = (bf16[64,128]{1,0:T(8,128)(2,1)S(1)}, bf16[64,128]{1,0:T(8,128)(2,1)S(1)}, u32[]{:S(2)}, u32[]{:S(2)}) collective-permute-start(bf16[64,128]{1,0:T(8,128)(2,1)S(1)} %get-tuple-element.145), channel_id=1, source_target_pairs={{0,16},{1,17},{2,18},{3,19},{4,20},{5,21},{6,22},{7,23},{8,24},{9,... | collective-permute-start | bytes 49160 | tf_op jit(solution)/shard_map/while/body/eval_jaxpr/ppermute | solution.py:31
  75.4 3.8 %collective-permute-start.2 = (bf16[1,64,128]{2,1,0:T(8,128)(2,1)S(1)}, bf16[1,64,128]{2,1,0:T(8,128)(2,1)S(1)}, u32[]{:S(2)}, u32[]{:S(2)}) collective-permute-start(bf16[1,64,128]{2,1,0:T(8,128)(2,1)S(1)} %bitcast.58), channel_id=1, source_target_pairs={{0,2},{2,0},{4,6},{6,4},{8,10},{10,8},{12,14},{14,12},{1,3},{3,1},... | collective-permute-start | bytes 49160 | tf_op jit(solution)/shard_map/ppermute | solution.py:17
  79.1 4.0 %collective-permute-start.3 = (bf16[2,64,128]{2,1,0:T(8,128)(2,1)S(1)}, bf16[2,64,128]{2,1,0:T(8,128)(2,1)S(1)}, u32[]{:S(2)}, u32[]{:S(2)}) collective-permute-start(bf16[2,64,128]{2,1,0:T(8,128)(2,1)S(1)} %pad_maximum_fusion.2), channel_id=1, source_target_pairs={{0,4},{2,6},{4,0},{6,2},{8,12},{10,14},{12,8},{14,10},{1,5},{3,7},... | collective-permute-start | bytes 98312 | tf_op jit(solution)/shard_map/ppermute | solution.py:17
  83.2 5.7 %collective-permute-start.4 = (bf16[4,64,128]{2,1,0:T(8,128)(2,1)S(1)}, bf16[4,64,128]{2,1,0:T(8,128)(2,1)S(1)}, u32[]{:S(2)}, u32[]{:S(2)}) collective-permute-start(bf16[4,64,128]{2,1,0:T(8,128)(2,1)S(1)} %pad_maximum_fusion.1), channel_id=1, source_target_pairs={{0,8},{2,10},{4,12},{6,14},{8,0},{10,2},{12,4},{14,6},{1,9},{3,11}... | collective-permute-start | bytes 196616 | tf_op jit(solution)/shard_map/ppermute | solution.py:17
  88.9 0.9 copy-start.2
  90.1 0.9 copy-start.1
  91.0 5.6 %collective-permute-start.1 = (bf16[64,128]{1,0:T(8,128)(2,1)S(1)}, bf16[64,128]{1,0:T(8,128)(2,1)S(1)}, u32[]{:S(2)}, u32[]{:S(2)}) collective-permute-start(bf16[64,128]{1,0:T(8,128)(2,1)S(1)} %get-tuple-element.160), channel_id=1, source_target_pairs={{16,0},{17,1},{18,2},{19,3},{20,4},{21,5},{22,6},{23,7},{24,8},{25... | collective-permute-start | bytes 49160 | tf_op jit(solution)/shard_map/while/body/eval_jaxpr/ppermute | solution.py:31
  127.7 5.6 %collective-permute-start.1 = (bf16[64,128]{1,0:T(8,128)(2,1)S(1)}, bf16[64,128]{1,0:T(8,128)(2,1)S(1)}, u32[]{:S(2)}, u32[]{:S(2)}) collective-permute-start(bf16[64,128]{1,0:T(8,128)(2,1)S(1)} %get-tuple-element.160), channel_id=1, source_target_pairs={{16,0},{17,1},{18,2},{19,3},{20,4},{21,5},{22,6},{23,7},{24,8},{25... | collective-permute-start | bytes 49160 | tf_op jit(solution)/shard_map/while/body/eval_jaxpr/ppermute | solution.py:31
  164.3 0.6 copy-start.3
